TPU v7x, 32 devices: a whole 2x2x4 slice. The times are simulated.
32 devices in a mesh: row: 8 (over z, x), col: 4 (over y, core).
Axes of the slice: x: 2, y: 2, z: 4, core: 2. Of those that a mesh axis runs over, the one named last changes fastest.
Arguments:
- curvature: float32 [32, 1024, 4096], P(None, 'row', 'col'), may hold values from -4 to 7, as said below
Outputs:
- factored: float32 [32, 1024, 4096], P(None, 'row', 'col')
Inputs may be any that keep to these rules, and one draw needn't show every extreme that they name: `curvature`: rows 0 to 4095, read as a square matrix, are symmetric positive definite with smallest eigenvalue at least 0.5.
All inputs are finite; a program needn't handle non-finite values.
Results may differ from a plain program's by a relative error of at most 0.0014.
Values may be sent and summed in bfloat16 or wider, within the bound.
A program may use at most 192 MiB of HBM per device.

v0:
```python
import jax
import jax.numpy as jnp
from jax import lax
from jax.sharding import PartitionSpec as P

STEPS = 2


def from_root(x, axis, root):
    mine = lax.axis_index(axis) == root
    return lax.psum(jnp.where(mine, x, jnp.zeros_like(x)), axis)


def contract(left_rows, right_rows):
    return lax.dot_general(
        left_rows, right_rows, (((1,), (1,)), ((), ())), preferred_element_type=jnp.float32
    )


def on_device(curvature):
    cycles, rows_tile, panel_width = curvature.shape
    row_index = lax.axis_index("row")
    col_index = lax.axis_index("col")
    current = curvature
    diag_piece = current[0]
    for step in range(STEPS):
        is_owner = col_index == step
        row_count = (cycles - step - 1) * rows_tile
        diag_block = lax.all_gather(diag_piece, "row", axis=0, tiled=True)

        def solve_panel(operands):
            block_in, lower_block = operands
            factor = jnp.linalg.cholesky(block_in)
            own_rows = lax.dynamic_slice_in_dim(factor, row_index * rows_tile, rows_tile, 0)
            identity = jnp.eye(panel_width, dtype=jnp.float32)
            inverse = jax.scipy.linalg.solve_triangular(factor, identity, lower=True)
            solved = lax.dot_general(
                lower_block,
                inverse,
                (((1,), (1,)), ((), ())),
                precision=lax.Precision.HIGHEST,
                preferred_element_type=jnp.float32,
            )
            return (own_rows, solved)

        def skip_panel(operands):
            return (
                jnp.zeros((rows_tile, panel_width), jnp.float32),
                jnp.zeros((row_count, panel_width), jnp.float32),
            )

        own_rows, solved = lax.cond(
            is_owner,
            solve_panel,
            skip_panel,
            (diag_block, current[step + 1 :].reshape(row_count, panel_width)),
        )
        later_rows = from_root(solved.astype(jnp.bfloat16), "col", step)
        facing = jnp.clip(col_index - step - 1, 0, cycles - step - 2)
        own_block = lax.dynamic_slice_in_dim(later_rows, facing * rows_tile, rows_tile, 0)
        is_active = col_index > step
        below_old = current[step + 1 :]
        update = contract(later_rows, lax.all_gather(own_block, "row", axis=0, tiled=True))
        updated = below_old - update.reshape(cycles - step - 1, rows_tile, panel_width)
        next_piece = jnp.where(is_active, updated[0], below_old[0])
        current = current.at[step + 1 :].set(jnp.where(is_active, updated, below_old))
        owner_panel = jnp.concatenate(
            [
                jnp.zeros((step, rows_tile, panel_width), jnp.float32),
                own_rows[None],
                solved.reshape(cycles - step - 1, rows_tile, panel_width),
            ],
            0,
        )
        current = jnp.where(is_owner, owner_panel, current)
        diag_piece = next_piece
    cycle_ids = lax.broadcasted_iota(jnp.int32, (cycles, 1, 1), 0)
    blanked = (cycle_ids < STEPS) & (col_index >= STEPS)
    return jnp.where(blanked, jnp.zeros_like(current), current)


def solution(mesh):
    in_specs = (P(None, "row", "col"),)
    out_specs = P(None, "row", "col")
    return jax.shard_map(
        on_device, mesh=mesh, in_specs=in_specs, out_specs=out_specs, check_vma=False
    )
```

profile of v0, /device:TPU:0, one launch (start us, length us, event | category | flops | bytes accessed | tf_op | source)
XLA Modules:
  0.0 1494.5 jit_solution(17995090701722447400)
XLA Ops:
  8.7 11.8 slice.234
  20.5 66.3 %all-gather.11.cloned.1.call-done = f32[1,1024,1024]{1,2,0:T(8,128)} async-done(((f32[1,128,1024]{1,2,0:T(8,128)}), f32[1,1024,1024]{1,2,0:T(8,128)}) %all-gather.11.cloned.1.call-update) | async-done | bytes 4194320 | tf_op jit(solution)/shard_map/all_gather | solution.py:29
  86.8 428.6 %conditional.2 = (f32[1,128,1024]{2,1,0:T(8,128)S(1)}, bf16[3968,1024]{0,1:T(8,128)(2,1)}, f32[31,128,1024]{2,1,0:T(8,128)}) conditional(s32[]{:T(128)} %convert_element_type.33, () %tuple.48, (f32[1024,1024]{0,1:T(8,128)}, s32[]{:T(128)}, f32[31,128,1024]{2,1,0:T(8,128)}) %tuple.185), branch_computations={%region_0.0_spmd, %region_1.20_spmd} | conditional | flops 60012396544 | bytes 264643136 | solution.py:52
  86.8 5.5 copy.8
  92.3 4.4 fusion
  98.6 11.7 cholesky.619
  110.4 9.8 custom-call.55
  120.2 2.5 cholesky.645
  126.6 11.9 cholesky.638
  141.1 9.8 custom-call.56
  154.3 11.7 cholesky.659
  167.8 9.8 custom-call.57
  181.2 12.1 cholesky.678
  195.1 9.8 custom-call.58
  208.3 11.7 cholesky.697
  221.8 10.0 custom-call.59
  235.1 11.7 cholesky.716
  248.6 9.8 custom-call.60
  261.5 12.1 cholesky.735
  275.4 9.8 custom-call.61
  287.8 11.7 cholesky.752
  301.6 6.6 fusion.1
  308.2 23.8 %while.6 = (s32[]{:T(128)}, f32[1024,1024]{1,0:T(8,128)}, s32[8,2]{0,1:T(2,128)S(1)}, f32[8,128,128]{2,1,0:T(8,128)S(1)}, s32[]{:T(128)}) while((s32[]{:T(128)}, f32[1024,1024]{1,0:T(8,128)}, s32[8,2]{0,1:T(2,128)S(1)}, f32[8,128,128]{2,1,0:T(8,128)S(1)}, s32[]{:T(128)}) %tuple.166), condition=%wide.while_cond.2, body=%wide.while_body.2.sunk | while | flops 2 | bytes 131181 | solution.py:36
  332.1 78.8 %custom-call.62 = f32[8,128,128]{1,2,0:T(8,128)S(1)} custom-call(f32[8,128,128]{2,1,0:T(8,128)S(1)} %get-tuple-element.101), custom_call_target="InvertDiagBlocksLowerTriangular" | custom-call | tf_op jit(solution)/shard_map/cond/branch_1_fun/jit(_solve_triangular)/triangular_solve | solution.py:36
  419.6 2.4 fusion.20
  422.7 2.8 convolution_subtract_fusion.2
  426.2 2.8 convolution_subtract_fusion.1
  429.7 3.6 convolution_subtract_fusion.3
  435.9 61.5 %fusion.146 = (bf16[3968,1024]{0,1:T(8,128)(2,1)}, f32[3968,1024]{0,1:T(8,128)}) fusion(f32[1024,1024]{1,0:T(8,128)} %copy-done.2, f32[3968,1024]{1,0:T(8,128)S(1)} %bitcast.232), kind=kOutput, calls=%fused_computation.337 | convolution fusion | flops 49933058048 | bytes 44826624 | tf_op jit(solution)/shard_map/cond/branch_1_fun/dot_general | solution.py:37
  497.4 16.7 %copy.9 = f32[3968,1024]{1,0:T(8,128)} copy(f32[3968,1024]{0,1:T(8,128)} %get-tuple-element.189) | data formatting | bytes 32505856 | tf_op jit(solution)/shard_map/cond/branch_1_fun/dot_general | solution.py:37
  515.4 7.3 broadcast_select_fusion
  522.8 146.0 %all-reduce.4.cloned.1.call-done = bf16[3968,1024]{0,1:T(8,128)(2,1)} async-done(((bf16[3968,1024]{0,1:T(8,128)(2,1)}), bf16[3968,1024]{0,1:T(8,128)(2,1)}) %all-reduce.4.cloned.1.call-update) | async-done | bytes 8126480 | tf_op jit(solution)/shard_map/psum | solution.py:11
  670.5 12.0 copy.108
  682.5 38.9 %all-gather.7.cloned.1.call-done = bf16[1024,1024]{0,1:T(8,128)(2,1)} async-done(((bf16[128,1024]{0,1:T(8,128)(2,1)}), bf16[1024,1024]{0,1:T(8,128)(2,1)}) %all-gather.7.cloned.1.call-update) | async-done | bytes 2097168 | tf_op jit(solution)/shard_map/all_gather | solution.py:63
  721.3 15.7 %fusion.148 = f32[3968,1024]{1,0:T(8,128)} fusion(bf16[3968,1024]{0,1:T(8,128)(2,1)} %all-reduce.4.cloned.1.call-done, bf16[1024,1024]{0,1:T(8,128)(2,1)} %all-gather.7.cloned.1.call-done), kind=kOutput, calls=%fused_computation.339 | convolution fusion | flops 8321499136 | bytes 26476544 | tf_op jit(solution)/shard_map/dot_general | solution.py:15
  737.0 16.9 %select_dynamic-update-slice_fusion = (f32[32,128,1024]{2,1,0:T(8,128)}, f32[31,128,1024]{2,1,0:T(8,128)S(1)}) fusion(f32[32,128,1024]{2,1,0:T(8,128)} %copy.108, pred[]{:T(512)S(6)} %gt.6, f32[31,128,1024]{2,1,0:T(8,128)} %bitcast.229), kind=kLoop, calls=%fused_computation.326 | loop fusion | flops 8126464 | bytes 65011712 | tf_op jit(solution)/shard_map/scatter | solution.py:66
  755.8 13.5 maximum_select_fusion
  769.3 14.6 slice.253
  783.9 43.0 %all-gather.13.cloned.1.call-done = f32[1,1024,1024]{2,1,0:T(8,128)} async-done(((f32[1,128,1024]{2,1,0:T(8,128)}), f32[1,1024,1024]{2,1,0:T(8,128)}) %all-gather.13.cloned.1.call-update) | async-done | bytes 4194320 | tf_op jit(solution)/shard_map/all_gather | solution.py:29
  826.9 16.6 %conditional.3 = (f32[1,128,1024]{2,1,0:T(8,128)S(1)}, f32[30,128,1024]{2,1,0:T(8,128)}, bf16[3840,1024]{0,1:T(8,128)(2,1)}) conditional(s32[]{:T(128)} %convert_element_type.32, () %tuple.47, (f32[1024,1024]{1,0:T(8,128)}, s32[]{:T(128)}, f32[30,128,1024]{2,1,0:T(8,128)}) %tuple.186), branch_computations={%region_19.22_spmd, %region_20.23_spmd} | conditional | flops 58401652736 | bytes 243933728 | solution.py:52
  826.9 7.5 reshape.156
  834.4 3.7 broadcast.321
  843.5 3.7 broadcast_select_fusion.1
  847.3 546.5 %all-reduce.6.cloned.1.call-done = bf16[3840,1024]{0,1:T(8,128)(2,1)} async-done(((bf16[3840,1024]{0,1:T(8,128)(2,1)}), bf16[3840,1024]{0,1:T(8,128)(2,1)}) %all-reduce.6.cloned.1.call-update) | async-done | bytes 7864336 | tf_op jit(solution)/shard_map/psum | solution.py:11
  1395.5 50.8 %all-gather.9.cloned.1.call-done = bf16[1024,1024]{0,1:T(8,128)(2,1)} async-done(((bf16[128,1024]{0,1:T(8,128)(2,1)}), bf16[1024,1024]{0,1:T(8,128)(2,1)}) %all-gather.9.cloned.1.call-update) | async-done | bytes 2097168 | tf_op jit(solution)/shard_map/all_gather | solution.py:63
  1446.3 11.5 fusion.149
  1457.8 12.2 fusion.143
  1470.1 17.3 %fusion.142 = f32[32,128,1024]{2,1,0:T(8,128)} fusion(f32[32,128,1024]{2,1,0:T(8,128)} %fusion.143, f32[30,128,1024]{2,1,0:T(8,128)} %get-tuple-element.85, f32[1,128,1024]{2,1,0:T(8,128)S(1)} %get-tuple-element.84, f32[32]{0:T(128)S(1)} %pad.25.clone, pred[32]{0:T(512)(128)(4,1)S(1)} %compare_and_fusion, pred[]{:T(512)S(6)} %eq.16), kind=kLoop, calls=%fused_computation.325 | loop fusion | flops 16777216 | bytes 49807520 | tf_op jit(solution)/shard_map/jit(_where)/select_n | solution.py:79
  (109 shorter events, 79.8 us)
Async XLA Ops:
  6.5 80.2 %all-gather.11.cloned.1.call-start = ((), (), s32[]{:S(2)}) async-start(), calls=%async_computation.4 | async-start | bytes 4718592 | tf_op jit(solution)/shard_map/all_gather | solution.py:29
  8.6 660.1 %all-reduce.4.cloned.1.call-start = ((), (), s32[]{:S(2)}) async-start(), calls=%async_computation | async-start | bytes 16252928 | tf_op jit(solution)/shard_map/psum | solution.py:11
  96.7 1.9 copy-start
  416.6 19.2 %slice-start = ((s8[16252928]{0:T(1024)(128)(4,1)}), s8[4194304]{0:T(1024)(128)(4,1)S(1)}, s32[]{:S(2)}) async-start(s8[16252928]{0:T(1024)(128)(4,1)} %bitcast.230), calls=%async_computation.6 | async-start | bytes 8388608 | tf_op jit(solution)/shard_map/cond
  419.6 16.3 %slice-start.1 = ((s8[16252928]{0:T(1024)(128)(4,1)}), s8[4194304]{0:T(1024)(128)(4,1)S(1)}, s32[]{:S(2)}) async-start(s8[16252928]{0:T(1024)(128)(4,1)} %bitcast.230), calls=%async_computation.7 | async-start | bytes 8388608 | tf_op jit(solution)/shard_map/cond
  422.7 13.2 slice-start.2
  429.0 6.8 slice-start.3
  433.9 2.0 copy-start.2
  522.7 198.6 %all-gather.7.cloned.1.call-start = ((), (), s32[]{:S(2)}) async-start(), calls=%async_computation.1 | async-start | bytes 2359296 | tf_op jit(solution)/shard_map/all_gather | solution.py:63
  670.4 156.5 %all-gather.13.cloned.1.call-start = ((), (), s32[]{:S(2)}) async-start(), calls=%async_computation.5 | async-start | bytes 4718592 | tf_op jit(solution)/shard_map/all_gather | solution.py:29
  755.8 638.0 %all-reduce.6.cloned.1.call-start = ((), (), s32[]{:S(2)}) async-start(), calls=%async_computation.2 | async-start | bytes 15728640 | tf_op jit(solution)/shard_map/psum | solution.py:11
  847.2 599.1 %all-gather.9.cloned.1.call-start = ((), (), s32[]{:S(2)}) async-start(), calls=%async_computation.3 | async-start | bytes 2359296 | tf_op jit(solution)/shard_map/all_gather | solution.py:63
Sparse Core Ops, SparseCore 0:
  9.4 77.3 all-gather.10
  522.8 145.8 all-reduce.3
  670.8 50.4 all-gather.6
  755.9 70.9 all-gather.12
  847.3 546.3 all-reduce.5
  1395.7 50.6 all-gather.8
where the time goes:
time: 1500 us; the launch traced here: 1490 us
  waiting for transfers between devices  892 us (59%)
  other arithmetic  335 us (22%)
  matrix products  134 us (9%)
  local copies, waits for them, and re-layouts  108 us (7%)
    psum x2, waiting for transfers between devices, from_root(): return lax.psum(jnp.where(mine, x, jnp.zeros_like(x)), axis)  693 us
    another operation x30, other arithmetic, solve_panel(): factor = jnp.linalg.cholesky(block_in)  172 us
    all_gather x2, waiting for transfers between devices, on_device(): diag_block = lax.all_gather(diag_piece, 'row', axis=0, tiled=True)  109 us
    all_gather x2, waiting for transfers between devices, on_device(): lax.all_gather(own_block, 'row', axis=0, tiled=True)  89.7 us
    another operation x4, other arithmetic, solve_panel(): inverse = jax.scipy.linalg.solve_triangular(factor, identity, lower=True)  85.4 us
    dot_general x1, matrix products, solve_panel(): lax.dot_general(lower_block, inverse, (((1,), (1,)), ((), ())), precision...  61.5 us
  transfers between devices with their start and end apart: 6, of which 6 were waited for; matrix products, arithmetic and copies ran while one was open for 3% of the time, Pallas kernels for 0%

commit v1 on v0

v1 whole, which is shorter than its diff:
```python
import jax
import jax.numpy as jnp
from jax import lax
from jax.sharding import PartitionSpec as P

BLOCK = 128
HIGH = lax.Precision.HIGH
HIGHEST = lax.Precision.HIGHEST


def from_root(x, axis, root):
    mine = lax.axis_index(axis) == root
    return lax.psum(jnp.where(mine, x, jnp.zeros_like(x)), axis)


def nt(left, right, precision=None):
    return lax.dot_general(
        left,
        right,
        (((1,), (1,)), ((), ())),
        precision=precision,
        preferred_element_type=jnp.float32,
    )


def nn(left, right):
    return lax.dot_general(
        left,
        right,
        (((1,), (0,)), ((), ())),
        precision=HIGHEST,
        preferred_element_type=jnp.float32,
    )


def factor_and_inverse(block):
    n = block.shape[0]
    width = min(BLOCK, n)
    rest = 0.5 * (block + block.T)
    identity = jnp.eye(width, dtype=jnp.float32)
    columns, inverses = [], []
    for start in range(0, n, width):
        small = lax.linalg.cholesky(rest[:width, :width], symmetrize_input=False)
        inverse = jax.scipy.linalg.solve_triangular(small, identity, lower=True)
        inverses.append(inverse)
        pieces = [jnp.zeros((start, width), jnp.float32)] if start else []
        pieces.append(small)
        if start + width < n:
            below = nt(rest[width:, :width], inverse, HIGHEST)
            rest = rest[width:, width:] - nt(below, below, HIGHEST)
            pieces.append(below)
        columns.append(jnp.concatenate(pieces, 0))
    factor = jnp.concatenate(columns, 1)
    size = width
    while len(inverses) > 1:
        merged = []
        for i in range(0, len(inverses), 2):
            top, bottom = inverses[i], inverses[i + 1]
            at = i * size
            corner = factor[at + size : at + 2 * size, at : at + size]
            left = -nn(bottom, nn(corner, top))
            merged.append(
                jnp.concatenate(
                    [
                        jnp.concatenate([top, jnp.zeros_like(top)], 1),
                        jnp.concatenate([left, bottom], 1),
                    ],
                    0,
                )
            )
        inverses = merged
        size *= 2
    return factor, inverses[0]


def on_device(curvature):
    cycles, tile, width = curvature.shape
    row = lax.axis_index("row")
    col = lax.axis_index("col")

    def gather_rows(piece):
        return lax.all_gather(piece, "row", axis=0, tiled=True)

    def own_rows(matrix):
        return lax.dynamic_slice_in_dim(matrix, row * tile, tile, 0)

    block00 = gather_rows(from_root(curvature[0], "col", 0))
    head = from_root(jnp.stack([curvature[0], curvature[1]], 0), "col", 1)
    block01 = gather_rows(head[0])
    block11 = gather_rows(head[1])
    mine0 = gather_rows(curvature[0])
    mine1 = gather_rows(curvature[1])

    factor0, inverse0 = factor_and_inverse(block00)
    below = curvature[1:].reshape((cycles - 1) * tile, width)
    solved0 = nt(below, inverse0, HIGH)
    sent0 = solved0.astype(jnp.bfloat16)
    sent0, block11, block01 = lax.optimization_barrier((sent0, block11, block01))
    panel0 = from_root(sent0, "col", 0)

    next0 = nn(inverse0, block01).astype(jnp.bfloat16)
    facing0 = nn(inverse0, mine0).astype(jnp.bfloat16)

    def tn(left, right):
        return lax.dot_general(
            left, right, (((0,), (0,)), ((), ())), preferred_element_type=jnp.float32
        )

    factor1, inverse1 = factor_and_inverse(block11 - tn(next0, next0))
    facing1 = nn(inverse1, mine1 - tn(next0, facing0)).astype(jnp.bfloat16)

    def plain(left, right):
        return lax.dot_general(
            left, right, (((1,), (0,)), ((), ())), preferred_element_type=jnp.float32
        )

    state = jnp.where(col == 0, solved0, below - plain(panel0, facing0))
    low = state[tile:]
    solved1 = nt(low, inverse1, HIGH)
    panel1 = from_root(solved1.astype(jnp.bfloat16), "col", 1)
    low = jnp.where(
        col == 1, solved1, jnp.where(col > 1, low - plain(panel1, facing1), low)
    )
    zeros = jnp.zeros((tile, width), jnp.float32)
    first = jnp.where(col == 0, own_rows(factor0), zeros)
    second = jnp.where(
        col == 0, state[:tile], jnp.where(col == 1, own_rows(factor1), zeros)
    )
    return jnp.concatenate([first, second, low], 0).reshape(cycles, tile, width)


def solution(mesh):
    in_specs = (P(None, "row", "col"),)
    out_specs = P(None, "row", "col")
    return jax.shard_map(
        on_device, mesh=mesh, in_specs=in_specs, out_specs=out_specs, check_vma=False
    )
```

time: 1500 us -> 993 us (0.66)
  waiting for transfers between devices: 892 us -> 221 us
  matrix products: 134 us -> 255 us
  other arithmetic: 335 us -> 427 us
  local copies, waits for them, and re-layouts: 108 us -> 59.1 us
    psum x2 -> x3, waiting for transfers between devices: 693 us -> 157 us  [from_root(): return lax.psum(jnp.where(mine, x, jnp.zeros_like(x)), axis)]
    dot_general x3 -> x65, matrix products: 88.7 us -> 247 us  [the longest x30 117 us: nt(): lax.dot_general(left, right, (((1,), (1,)), ((), ())), precision=precisio...]
    all_gather x4 -> x5, waiting for transfers between devices: 199 us -> 61.3 us  [gather_rows(): return lax.all_gather(piece, 'row', axis=0, tiled=True)]
    another operation x34 -> x80, other arithmetic: 258 us -> 389 us  [the longest x48 207 us: factor_and_inverse(): small = lax.linalg.cholesky(rest[:width, :width], symmetrize_input=False)]
    another operation x29 -> x16, matrix products: 45.5 us -> 7.73 us  [factor_and_inverse(): inverse = jax.scipy.linalg.solve_triangular(small, identity, lower=True)]
    select_n x3 -> x2, other arithmetic: 32.7 us -> 1.35 us  [the longest x1 1.32 us: on_device(): jnp.where(col == 0, state[:tile], jnp.where(col == 1, own_rows(factor1),...]
    another operation x35 -> x16, local copies, waits for them, and re-layouts: 35.4 us -> 6.28 us  [the longest x8 6.2 us: factor_and_inverse(): inverse = jax.scipy.linalg.solve_triangular(small, identity, lower=True)]
    scatter x2 -> x0, other arithmetic: 29.1 us -> none  [on_device(): current.at[step + 1:].set(jnp.where(is_active, updated, below_old))]
  transfers between devices with their start and end apart: 6 -> 8, of which waited for: 6 -> 3; matrix products, arithmetic and copies ran while one was open for 3% -> 70% of each run, Pallas kernels for 0% -> 0%
where the time goes in v1:
time: 993 us; the launch traced here: 978 us
  other arithmetic  427 us (43%)
  matrix products  255 us (26%)
  waiting for transfers between devices  221 us (22%)
  local copies, waits for them, and re-layouts  59.1 us (6%)
  between operations  16 us (2%)
    another operation x48, other arithmetic, factor_and_inverse(): small = lax.linalg.cholesky(rest[:width, :width], symmetrize_input=False)  207 us
    another operation x32, other arithmetic, factor_and_inverse(): inverse = jax.scipy.linalg.solve_triangular(small, identity, lower=True)  183 us
    psum x3, waiting for transfers between devices, from_root(): return lax.psum(jnp.where(mine, x, jnp.zeros_like(x)), axis)  157 us
    dot_general x30, matrix products, nt(): lax.dot_general(left, right, (((1,), (1,)), ((), ())), precision=precisio...  117 us
    dot_general x31, matrix products, nn(): lax.dot_general(left, right, (((1,), (0,)), ((), ())), precision=HIGHEST,...  81.6 us
    all_gather x5, waiting for transfers between devices, gather_rows(): return lax.all_gather(piece, 'row', axis=0, tiled=True)  61.3 us
    dot_general x2, matrix products, plain(): lax.dot_general(left, right, (((1,), (0,)), ((), ())), preferred_element_...  40.1 us
    unnamed x196, local copies, waits for them, and re-layouts  22.1 us
  transfers between devices with their start and end apart: 8, of which 3 were waited for; matrix products, arithmetic and copies ran while one was open for 70% of the time, Pallas kernels for 0%

profile of v1, /device:TPU:0, one launch (start us, length us, event | category | flops | bytes accessed | tf_op | source)
XLA Modules:
  0.0 978.4 jit_solution(16894256061563243643)
XLA Ops:
  11.2 45.7 %all-reduce.25.cloned.1.call-done = (f32[128,1024]{0,1:T(8,128)}, f32[2,128,1024]{1,2,0:T(8,128)}) async-done(((f32[128,1024]{0,1:T(8,128)}, f32[2,128,1024]{1,2,0:T(8,128)}), (f32[128,1024]{0,1:T(8,128)}, f32[2,128,1024]{1,2,0:T(8,128)})) %all-reduce.25.cloned.1.call-update) | async-done | bytes 1572880 | tf_op jit(solution)/shard_map/psum | solution.py:13
  60.5 11.9 %slice.227 = f32[31,128,1024]{2,1,0:T(8,128)} slice(f32[32,128,1024]{2,1,0:T(8,128)} %param.4), slice={[1:32], [0:128], [0:1024]} | slice | bytes 32505856 | tf_op jit(solution)/shard_map/slice | solution.py:95
  72.4 61.3 %all-gather.10.cloned.1.call-done = f32[1024,1024]{0,1:T(8,128)} async-done(((f32[128,1024]{0,1:T(8,128)}), f32[1024,1024]{0,1:T(8,128)}) %all-gather.10.cloned.1.call-update) | async-done | bytes 4194320 | tf_op jit(solution)/shard_map/all_gather | solution.py:82
  133.7 5.3 copy.3
  145.9 11.7 %custom-call.36 = f32[128,128]{1,0:T(8,128)S(1)} custom-call(f32[128,128]{1,0:T(8,128)S(1)} %slice.260), custom_call_target="Cholesky" | custom-call | tf_op jit(solution)/shard_map/cholesky/custom-call.1 | solution.py:43
  158.9 9.8 %custom-call.37 = f32[1,128,128]{1,2,0:T(8,128)S(1)} custom-call(f32[1,128,128]{2,1,0:T(8,128)S(1)} %get-tuple-element.45), custom_call_target="InvertDiagBlocksLowerTriangular" | custom-call | tf_op jit(solution)/shard_map/jit(_solve_triangular)/triangular_solve | solution.py:44
  170.6 4.9 slice_subtract_fusion.1
  177.2 12.0 %custom-call.38 = f32[128,128]{1,0:T(8,128)S(1)} custom-call(f32[128,128]{1,0:T(8,128)S(1)} %slice.263), custom_call_target="Cholesky" | custom-call | tf_op jit(solution)/shard_map/cholesky/custom-call.1 | solution.py:43
  190.7 9.8 %custom-call.39 = f32[1,128,128]{1,2,0:T(8,128)S(1)} custom-call(f32[1,128,128]{2,1,0:T(8,128)S(1)} %get-tuple-element.43), custom_call_target="InvertDiagBlocksLowerTriangular" | custom-call | tf_op jit(solution)/shard_map/jit(_solve_triangular)/triangular_solve | solution.py:44
  207.4 11.7 %custom-call.40 = f32[128,128]{1,0:T(8,128)S(1)} custom-call(f32[128,128]{1,0:T(8,128)S(1)} %slice.266), custom_call_target="Cholesky" | custom-call | tf_op jit(solution)/shard_map/cholesky/custom-call.1 | solution.py:43
  221.1 10.0 %custom-call.41 = f32[1,128,128]{1,2,0:T(8,128)S(1)} custom-call(f32[1,128,128]{2,1,0:T(8,128)S(1)} %get-tuple-element.41), custom_call_target="InvertDiagBlocksLowerTriangular" | custom-call | tf_op jit(solution)/shard_map/jit(_solve_triangular)/triangular_solve | solution.py:44
  236.9 11.7 %custom-call.42 = f32[128,128]{1,0:T(8,128)S(1)} custom-call(f32[128,128]{1,0:T(8,128)S(1)} %slice.269), custom_call_target="Cholesky" | custom-call | tf_op jit(solution)/shard_map/cholesky/custom-call.1 | solution.py:43
  250.6 9.8 %custom-call.43 = f32[1,128,128]{1,2,0:T(8,128)S(1)} custom-call(f32[1,128,128]{2,1,0:T(8,128)S(1)} %get-tuple-element.39), custom_call_target="InvertDiagBlocksLowerTriangular" | custom-call | tf_op jit(solution)/shard_map/jit(_solve_triangular)/triangular_solve | solution.py:44
  264.3 11.9 %custom-call.44 = f32[128,128]{1,0:T(8,128)S(1)} custom-call(f32[128,128]{1,0:T(8,128)S(1)} %slice.272), custom_call_target="Cholesky" | custom-call | tf_op jit(solution)/shard_map/cholesky/custom-call.1 | solution.py:43
  277.5 9.8 %custom-call.45 = f32[1,128,128]{1,2,0:T(8,128)S(1)} custom-call(f32[1,128,128]{2,1,0:T(8,128)S(1)} %get-tuple-element.37), custom_call_target="InvertDiagBlocksLowerTriangular" | custom-call | tf_op jit(solution)/shard_map/jit(_solve_triangular)/triangular_solve | solution.py:44
  291.4 11.7 %custom-call.46 = f32[128,128]{1,0:T(8,128)S(1)} custom-call(f32[128,128]{1,0:T(8,128)S(1)} %slice.275), custom_call_target="Cholesky" | custom-call | tf_op jit(solution)/shard_map/cholesky/custom-call.1 | solution.py:43
  304.4 9.8 %custom-call.47 = f32[1,128,128]{1,2,0:T(8,128)S(1)} custom-call(f32[1,128,128]{2,1,0:T(8,128)S(1)} %get-tuple-element.35), custom_call_target="InvertDiagBlocksLowerTriangular" | custom-call | tf_op jit(solution)/shard_map/jit(_solve_triangular)/triangular_solve | solution.py:44
  317.4 11.7 %custom-call.48 = f32[128,128]{1,0:T(8,128)S(1)} custom-call(f32[128,128]{1,0:T(8,128)S(1)} %slice.278), custom_call_target="Cholesky" | custom-call | tf_op jit(solution)/shard_map/cholesky/custom-call.1 | solution.py:43
  331.1 9.8 %custom-call.49 = f32[1,128,128]{1,2,0:T(8,128)S(1)} custom-call(f32[1,128,128]{2,1,0:T(8,128)S(1)} %get-tuple-element.33), custom_call_target="InvertDiagBlocksLowerTriangular" | custom-call | tf_op jit(solution)/shard_map/jit(_solve_triangular)/triangular_solve | solution.py:44
  341.8 11.7 %custom-call.50 = f32[128,128]{1,0:T(8,128)S(1)} custom-call(f32[128,128]{1,0:T(8,128)S(1)} %convolution_subtract_fusion.8), custom_call_target="Cholesky" | custom-call | tf_op jit(solution)/shard_map/cholesky/custom-call.1 | solution.py:43
  357.0 9.9 %custom-call.51 = f32[1,128,128]{1,2,0:T(8,128)S(1)} custom-call(f32[1,128,128]{2,1,0:T(8,128)S(1)} %get-tuple-element.31), custom_call_target="InvertDiagBlocksLowerTriangular" | custom-call | tf_op jit(solution)/shard_map/jit(_solve_triangular)/triangular_solve | solution.py:44
  377.7 31.0 %bitcast_convert_fusion = (bf16[3968,1024]{1,0:T(8,128)(2,1)}, f32[1024,3968]{0,1:T(8,128)}) fusion(f32[3968,1024]{1,0:T(8,128)} %bitcast.189, f32[512,512]{1,0:T(8,128)S(1)} %select_maximum_fusion.3, f32[128,128]{1,0:T(8,128)S(1)} %copy-done.83, f32[128,128]{1,0:T(8,128)S(1)} %convolution_negate_fusion.10, f32[128,256]{1,0:T(8,128)S(1)} %copy-done.64, ...), kind=kOutput, calls=%fused_computation.3 | convolution fusion | flops 24976949248 | bytes 43778048 | tf_op jit(solution)/shard_map/dot_general | solution.py:17
  408.7 7.1 broadcast_select_fusion
  416.7 20.2 %convolution_convert_fusion = bf16[1024,1024]{1,0:T(8,128)(2,1)S(1)} fusion(f32[1024,1024]{0,1:T(8,128)} %bitcast.192, f32[512,512]{1,0:T(8,128)} %copy-done.31, f32[128,128]{1,0:T(8,128)S(1)} %copy-done.84, f32[128,128]{1,0:T(8,128)S(1)} %convolution_negate_fusion.10, f32[128,256]{1,0:T(8,128)S(1)} %copy-done.65, ...), kind=kOutput, calls=%fused_computation.27 | convolution fusion | flops 12894339072 | bytes 9437184 | tf_op jit(solution)/shard_map/dot_general | solution.py:27
  442.8 5.6 copy.18
  455.2 11.7 %custom-call.52 = f32[128,128]{1,0:T(8,128)S(1)} custom-call(f32[128,128]{1,0:T(8,128)S(1)} %slice.287), custom_call_target="Cholesky" | custom-call | tf_op jit(solution)/shard_map/cholesky/custom-call.1 | solution.py:43
  468.7 9.8 %custom-call.53 = f32[1,128,128]{1,2,0:T(8,128)S(1)} custom-call(f32[1,128,128]{2,1,0:T(8,128)S(1)} %get-tuple-element.29), custom_call_target="InvertDiagBlocksLowerTriangular" | custom-call | tf_op jit(solution)/shard_map/jit(_solve_triangular)/triangular_solve | solution.py:44
  486.9 11.9 %custom-call.54 = f32[128,128]{1,0:T(8,128)S(1)} custom-call(f32[128,128]{1,0:T(8,128)S(1)} %slice.290), custom_call_target="Cholesky" | custom-call | tf_op jit(solution)/shard_map/cholesky/custom-call.1 | solution.py:43
  500.9 9.8 %custom-call.55 = f32[1,128,128]{1,2,0:T(8,128)S(1)} custom-call(f32[1,128,128]{2,1,0:T(8,128)S(1)} %get-tuple-element.27), custom_call_target="InvertDiagBlocksLowerTriangular" | custom-call | tf_op jit(solution)/shard_map/jit(_solve_triangular)/triangular_solve | solution.py:44
  518.4 11.7 %custom-call.56 = f32[128,128]{1,0:T(8,128)S(1)} custom-call(f32[128,128]{1,0:T(8,128)S(1)} %slice.293), custom_call_target="Cholesky" | custom-call | tf_op jit(solution)/shard_map/cholesky/custom-call.1 | solution.py:43
  532.1 10.2 %custom-call.57 = f32[1,128,128]{1,2,0:T(8,128)S(1)} custom-call(f32[1,128,128]{2,1,0:T(8,128)S(1)} %get-tuple-element.25), custom_call_target="InvertDiagBlocksLowerTriangular" | custom-call | tf_op jit(solution)/shard_map/jit(_solve_triangular)/triangular_solve | solution.py:44
  548.6 11.7 %custom-call.58 = f32[128,128]{1,0:T(8,128)S(1)} custom-call(f32[128,128]{1,0:T(8,128)S(1)} %slice.296), custom_call_target="Cholesky" | custom-call | tf_op jit(solution)/shard_map/cholesky/custom-call.1 | solution.py:43
  562.3 9.8 %custom-call.59 = f32[1,128,128]{1,2,0:T(8,128)S(1)} custom-call(f32[1,128,128]{2,1,0:T(8,128)S(1)} %get-tuple-element.23), custom_call_target="InvertDiagBlocksLowerTriangular" | custom-call | tf_op jit(solution)/shard_map/jit(_solve_triangular)/triangular_solve | solution.py:44
  578.4 11.9 %custom-call.60 = f32[128,128]{1,0:T(8,128)S(1)} custom-call(f32[128,128]{1,0:T(8,128)S(1)} %slice.299), custom_call_target="Cholesky" | custom-call | tf_op jit(solution)/shard_map/cholesky/custom-call.1 | solution.py:43
  592.4 9.8 %custom-call.61 = f32[1,128,128]{1,2,0:T(8,128)S(1)} custom-call(f32[1,128,128]{2,1,0:T(8,128)S(1)} %get-tuple-element.21), custom_call_target="InvertDiagBlocksLowerTriangular" | custom-call | tf_op jit(solution)/shard_map/jit(_solve_triangular)/triangular_solve | solution.py:44
  606.9 13.2 %custom-call.62 = f32[128,128]{1,0:T(8,128)} custom-call(f32[128,128]{1,0:T(8,128)} %slice.302), custom_call_target="Cholesky" | custom-call | tf_op jit(solution)/shard_map/cholesky/custom-call.1 | solution.py:43
  623.9 11.3 %custom-call.63 = f32[1,128,128]{1,2,0:T(8,128)} custom-call(f32[1,128,128]{2,1,0:T(8,128)} %get-tuple-element.19), custom_call_target="InvertDiagBlocksLowerTriangular" | custom-call | tf_op jit(solution)/shard_map/jit(_solve_triangular)/triangular_solve | solution.py:44
  641.0 13.2 %custom-call.64 = f32[128,128]{1,0:T(8,128)} custom-call(f32[128,128]{1,0:T(8,128)} %slice.305), custom_call_target="Cholesky" | custom-call | tf_op jit(solution)/shard_map/cholesky/custom-call.1 | solution.py:43
  657.6 11.3 %custom-call.65 = f32[1,128,128]{1,2,0:T(8,128)} custom-call(f32[1,128,128]{2,1,0:T(8,128)} %get-tuple-element.17), custom_call_target="InvertDiagBlocksLowerTriangular" | custom-call | tf_op jit(solution)/shard_map/jit(_solve_triangular)/triangular_solve | solution.py:44
  680.2 13.2 %custom-call.66 = f32[128,128]{1,0:T(8,128)} custom-call(f32[128,128]{1,0:T(8,128)} %convolution_subtract_fusion.7), custom_call_target="Cholesky" | custom-call | tf_op jit(solution)/shard_map/cholesky/custom-call.1 | solution.py:43
  697.0 11.6 %custom-call.67 = f32[1,128,128]{1,2,0:T(8,128)} custom-call(f32[1,128,128]{2,1,0:T(8,128)} %get-tuple-element.15), custom_call_target="InvertDiagBlocksLowerTriangular" | custom-call | tf_op jit(solution)/shard_map/jit(_solve_triangular)/triangular_solve | solution.py:44
  726.2 20.0 %fusion.9 = bf16[1024,1024]{1,0:T(8,128)(2,1)} fusion(f32[1,1024,1024]{1,2,0:T(8,128)} %all-gather.16.cloned.1.call-done, f32[512,512]{1,0:T(8,128)} %copy-done.31, f32[128,128]{1,0:T(8,128)} %copy.12, f32[128,128]{1,0:T(8,128)} %copy-done.77, f32[128,256]{1,0:T(8,128)} %concatenate.225, f32[256,256]{1,0:T(8,128)} %copy-done.71, f32[256,512]{1,0:T(8,128)} %copy-done.61, ...), kind=kOutput, calls=%fused_computation.26 | convolution fusion | flops 12894339072 | bytes 9437184 | tf_op jit(solution)/shard_map/dot_general | solution.py:27
  746.1 23.1 %bitcast_select_fusion = f32[3968,1024]{1,0:T(8,128)} fusion(f32[1024,3968]{0,1:T(8,128)} %get-tuple-element.64, f32[3968,1024]{1,0:T(8,128)} %bitcast.190, pred[]{:T(512)S(6)} %eq.47, bf16[3968,1024]{1,0:T(8,128)(2,1)} %all-reduce.21.cloned.1.call-done, bf16[1024,1024]{1,0:T(8,128)(2,1)} %fusion.9), kind=kOutput, calls=%fused_computation.2 | convolution fusion | flops 8329625600 | bytes 58982400 | tf_op jit(solution)/shard_map/dot_general | solution.py:113
  769.2 31.3 %convert_select_fusion = (bf16[3840,1024]{1,0:T(8,128)(2,1)}, f32[3840,1024]{1,0:T(8,128)}) fusion(pred[]{:T(512)S(6)} %eq.49, f32[512,512]{1,0:T(8,128)} %select_maximum_fusion.2, f32[128,128]{1,0:T(8,128)} %copy.27, f32[128,128]{1,0:T(8,128)} %copy-done.81, f32[128,256]{1,0:T(8,128)} %concatenate.258, f32[256,256]{1,0:T(8,128)} %copy-done.72, ...), kind=kOutput, calls=%fused_computation.8 | convolution fusion | flops 24175443968 | bytes 42467328 | tf_op jit(solution)/shard_map/dot_general | solution.py:17
  812.6 17.2 %fusion.3 = bf16[1024,1024]{1,0:T(8,128)(2,1)} fusion(f32[1024,1024]{1,0:T(8,128)} %fusion.249, f32[1,1024,1024]{2,1,0:T(8,128)} %all-gather.18.cloned.1.call-done, f32[512,512]{1,0:T(8,128)S(1)} %copy-done.32, f32[128,128]{1,0:T(8,128)S(1)} %copy-done.86, f32[128,128]{1,0:T(8,128)S(1)} %copy-done.82, f32[128,256]{1,0:T(8,128)S(1)} %copy-done.67, ...), kind=kOutput, calls=%fused_computation.13 | convolution fusion | flops 12894339072 | bytes 13631488 | tf_op jit(solution)/shard_map/dot_general | solution.py:27
  831.1 111.7 %all-reduce.23.cloned.1.call-done = bf16[3840,1024]{1,0:T(8,128)(2,1)} async-done(((bf16[3840,1024]{1,0:T(8,128)(2,1)}), bf16[3840,1024]{1,0:T(8,128)(2,1)}) %all-reduce.23.cloned.1.call-update) | async-done | bytes 7864336 | tf_op jit(solution)/shard_map/psum | solution.py:13
  942.8 17.1 %fusion = f32[3840,1024]{1,0:T(8,128)} fusion(f32[3840,1024]{1,0:T(8,128)} %get-tuple-element.66, f32[3968,1024]{1,0:T(8,128)} %bitcast_select_fusion, bf16[3840,1024]{1,0:T(8,128)(2,1)} %all-reduce.23.cloned.1.call-done, pred[]{:T(512)S(6)} %gt.3, pred[]{:T(512)S(6)} %eq.49, bf16[1024,1024]{1,0:T(8,128)(2,1)} %fusion.3), kind=kOutput, calls=%fused_computation.4 | convolution fusion | flops 8064860160 | bytes 57147392 | tf_op jit(solution)/shard_map/dot_general | solution.py:113
  959.9 11.2 %pad_maximum_fusion = f32[4096,1024]{1,0:T(8,128)} fusion(f32[3840,1024]{1,0:T(8,128)} %fusion, f32[128,1024]{1,0:T(8,128)S(1)} %slice_select_fusion, f32[128,1024]{1,0:T(8,128)S(1)} %dynamic-slice_select_fusion), kind=kLoop, calls=%fused_computation.1 | loop fusion | flops 8388608 | bytes 33554432 | tf_op jit(solution)/shard_map/concatenate | solution.py:129
  (398 shorter events, 182.9 us)
Async XLA Ops:
  6.5 50.4 %all-reduce.25.cloned.1.call-start = ((), (), s32[]{:S(2)}) async-start(), calls=%async_computation.7 | async-start | bytes 3145728 | tf_op jit(solution)/shard_map/psum | solution.py:13
  8.9 50.3 %copy-start.8 = (f32[1,128,1024]{1,2,0:T(8,128)}, f32[1,128,1024]{1,2,0:T(8,128)S(1)}, u32[]{:S(2)}) copy-start(f32[1,128,1024]{1,2,0:T(8,128)S(1)} %copy.46) | copy-start | bytes 1572868
  11.2 122.5 %all-gather.10.cloned.1.call-start = ((), (), s32[]{:S(2)}) async-start(), calls=%async_computation | async-start | bytes 4718592 | tf_op jit(solution)/shard_map/all_gather | solution.py:82
  57.0 351.8 %all-gather.12.cloned.1.call-start = ((), (), s32[]{:S(2)}) async-start(), calls=%async_computation.3 | async-start | bytes 4718592 | tf_op jit(solution)/shard_map/all_gather | solution.py:82
  59.3 349.5 %all-gather.14.cloned.1.call-start = ((), (), s32[]{:S(2)}) async-start(), calls=%async_computation.4 | async-start | bytes 4718592 | tf_op jit(solution)/shard_map/all_gather | solution.py:82
  59.8 666.3 %all-gather.16.cloned.1.call-start = ((), (), s32[]{:S(2)}) async-start(), calls=%async_computation.5 | async-start | bytes 4718592 | tf_op jit(solution)/shard_map/all_gather | solution.py:82
  60.4 685.7 %all-reduce.21.cloned.1.call-start = ((), (), s32[]{:S(2)}) async-start(), calls=%async_computation.1 | async-start | bytes 16252928 | tf_op jit(solution)/shard_map/psum | solution.py:13
  158.9 213.1 %copy-start.44 = (f32[128,128]{1,0:T(8,128)}, f32[128,128]{1,0:T(8,128)S(1)}, u32[]{:S(2)}) copy-start(f32[128,128]{1,0:T(8,128)S(1)} %get-tuple-element.46) | copy-start | bytes 196612
  190.7 178.4 %copy-start.45 = (f32[128,128]{1,0:T(8,128)}, f32[128,128]{1,0:T(8,128)S(1)}, u32[]{:S(2)}) copy-start(f32[128,128]{1,0:T(8,128)S(1)} %get-tuple-element.44) | copy-start | bytes 196612
  264.3 23.0 %copy-start.15 = (f32[512,512]{1,0:T(8,128)}, f32[512,512]{1,0:T(8,128)S(1)}, u32[]{:S(2)}) copy-start(f32[512,512]{1,0:T(8,128)S(1)} %convolution_subtract_fusion.2) | copy-start | bytes 3145732
  277.5 92.1 %copy-start.47 = (f32[128,128]{1,0:T(8,128)}, f32[128,128]{1,0:T(8,128)S(1)}, u32[]{:S(2)}) copy-start(f32[128,128]{1,0:T(8,128)S(1)} %get-tuple-element.38) | copy-start | bytes 196612
  304.4 66.5 %copy-start.40 = (f32[128,128]{1,0:T(8,128)}, f32[128,128]{1,0:T(8,128)S(1)}, u32[]{:S(2)}) copy-start(f32[128,128]{1,0:T(8,128)S(1)} %get-tuple-element.36) | copy-start | bytes 196612
  341.5 32.3 %copy-start.22 = (f32[128,128]{1,0:T(8,128)}, f32[128,128]{1,0:T(8,128)S(1)}, u32[]{:S(2)}) copy-start(f32[128,128]{1,0:T(8,128)S(1)} %fusion.208) | copy-start | bytes 196612
  355.1 13.6 %copy-start.57 = (f32[128,128]{1,0:T(8,128)}, f32[128,128]{1,0:T(8,128)S(1)}, u32[]{:S(2)}) copy-start(f32[128,128]{1,0:T(8,128)S(1)} %copy.10) | copy-start | bytes 196612
  368.5 8.2 copy-start.61
  369.1 4.8 copy-start.27
  371.9 4.8 copy-start.31
  374.4 42.2 %copy-start.77 = (f32[128,128]{1,0:T(8,128)}, f32[128,128]{1,0:T(8,128)S(1)}, u32[]{:S(2)}) copy-start(f32[128,128]{1,0:T(8,128)S(1)} %convolution_negate_fusion.10) | copy-start | bytes 196612
  374.8 41.8 %copy-start.71 = (f32[256,256]{1,0:T(8,128)}, f32[256,256]{1,0:T(8,128)S(1)}, u32[]{:S(2)}) copy-start(f32[256,256]{1,0:T(8,128)S(1)} %convolution_negate_fusion.4) | copy-start | bytes 786436
  415.9 396.7 %all-gather.18.cloned.1.call-start = ((), (), s32[]{:S(2)}) async-start(), calls=%async_computation.6 | async-start | bytes 4718592 | tf_op jit(solution)/shard_map/all_gather | solution.py:82
  416.6 526.2 %all-reduce.23.cloned.1.call-start = ((), (), s32[]{:S(2)}) async-start(), calls=%async_computation.2 | async-start | bytes 15728640 | tf_op jit(solution)/shard_map/psum | solution.py:13
  416.7 21.6 %copy-start.92 = (f32[1,1024,1024]{1,2,0:T(8,128)S(1)}, f32[1,1024,1024]{1,2,0:T(8,128)}, u32[]{:S(2)}) copy-start(f32[1,1024,1024]{1,2,0:T(8,128)} %all-gather.12.cloned.1.call-done) | copy-start | bytes 12582916
  478.8 7.5 copy-start.25
  511.0 21.1 %copy-start.35 = (f32[128,128]{0,1:T(8,128)}, f32[128,128]{0,1:T(8,128)S(1)}, u32[]{:S(2)}) copy-start(f32[128,128]{0,1:T(8,128)S(1)} %fusion.100) | copy-start | bytes 196612
  572.4 29.7 %copy-start.33 = (f32[128,128]{0,1:T(8,128)}, f32[128,128]{0,1:T(8,128)S(1)}, u32[]{:S(2)}) copy-start(f32[128,128]{0,1:T(8,128)S(1)} %fusion.96) | copy-start | bytes 196612
  711.9 6.1 copy-start.26
  711.9 6.1 copy-start.53
  711.9 6.1 copy-start.54
  711.9 7.2 copy-start.10
  711.9 7.2 copy-start.18
  711.9 7.2 copy-start.42
  711.9 7.2 copy-start.51
  711.9 7.2 copy-start.56
  711.9 7.6 copy-start.13
  711.9 7.6 copy-start.28
  712.0 7.6 copy-start.38
  712.0 7.6 copy-start.49
  712.0 7.6 copy-start.50
  712.0 7.6 copy-start.69
  712.0 7.6 copy-start.78
  712.0 7.6 copy-start.90
  714.2 8.2 copy-start.62
  808.1 4.5 copy-start.32
  808.1 4.5 copy-start.63
  808.1 4.5 copy-start.67
  808.1 4.5 copy-start.73
  808.1 4.5 copy-start.82
  808.1 4.5 copy-start.86
  (58 other events, 125.3 us)
Sparse Core Ops, SparseCore 0:
  11.3 45.5 all-reduce.24
  59.0 74.6 all-gather.9
  135.7 73.1 all-gather.11
  210.9 74.0 all-gather.13
  286.9 73.2 all-gather.15
  416.0 145.8 all-reduce.20
  563.9 72.9 all-gather.17
  800.6 142.1 all-reduce.22
